TPU v7x, 32 devices: a whole 2x2x4 slice. The times are simulated.
32 devices in a mesh: groups: 2 (over y), seq: 16 (over z, x, core).
Axes of the slice: x: 2, y: 2, z: 4, core: 2. Of those that a mesh axis runs over, the one named last changes fastest.
Arguments:
- hidden: bfloat16 [4, 4, 8192], P('groups', None, 'seq'), parts along dimension 0, may hold values from -1200 to 1200
- norm_gain: bfloat16 [8192], P('seq'), may hold values from 0.099609375 to 1.8984375
- q_weight: bfloat16 [8192, 8192], P('seq'), may hold values from -0.0625 to 0.0625
- kv_weight: bfloat16 [8192, 2048], P('seq'), may hold values from -0.0625 to 0.0625
- out_weight: bfloat16 [8192, 8192], P('seq'), may hold values from -0.09375 to 0.09375
- head_kind: int32 [8], replicated, may hold values from 0 to 1, as said below
- ret_keys: bfloat16 [4, 4, 32768, 128], P('groups', None, 'seq'), parts along dimension 0, may hold values from -600 to 600
- ret_values: bfloat16 [4, 4, 32768, 128], P('groups', None, 'seq'), parts along dimension 0, may hold values from -8 to 8
- stream_keys: bfloat16 [4, 4, 2048, 128], P('groups', None, 'seq'), parts along dimension 0, may hold values from -600 to 600
- stream_values: bfloat16 [4, 4, 2048, 128], P('groups', None, 'seq'), parts along dimension 0, may hold values from -8 to 8
- cache_len: int32 [4], P('groups'), parts along dimension 0, may hold values from 1 to 32768, as said below
- sink_len: int32 [4], P('groups'), parts along dimension 0, may hold values from 1 to 128, as said below
- window_len: int32 [4], P('groups'), parts along dimension 0, may hold values from 1 to 1920, as said below
Outputs:
- layer_output: bfloat16 [4, 4, 8192], P('groups', None, 'seq'), parts along dimension 0
- new_entries: bfloat16 [4, 4, 2048], P('groups'), parts along dimension 0
There are 2 independent parts, one for each index of `groups`. A program takes and returns all parts, laid end to end along the dimension named above; an argument that names none is the same for every part. Nothing has to cross between parts.
Inputs may be any that keep to these rules, and one draw needn't show every extreme that they name: `head_kind`: exactly 4 of the 8 entries are 1, the others 0. `cache_len`: in every draw some request has all 32768 positions filled. `sink_len`: in every draw some request holds 128 sink tokens. `window_len`: in every draw some request holds 1920 recent tokens.
All inputs are finite; a program needn't handle non-finite values.
Results may differ from a plain program's by a relative error of at most 0.0075.
The roundings to bfloat16 on the way count: a program that leaves them out, or rounds other values in their place, can miss the bound.
Values may be sent and summed in bfloat16 or wider, within the bound.
No kernel may reach another device: no remote copies, remote signals or barrier semaphores. Data moves between devices by JAX's collectives and lax.ppermute only.
A program may use at most 128 MiB of HBM per device.

v0:
```python
import jax
import jax.numpy as jnp
from jax import lax
from jax.sharding import PartitionSpec as P

SINK_CAP = 128


epsilon = 1e-05
floor_score = -1e30


def joined(part, axis, combine):
    gathered = jax.tree.map(lambda a: lax.all_gather(a, axis), part)

    def take(source):
        return jax.tree.map(lambda a: lax.dynamic_index_in_dim(a, source, 0, False), gathered)

    return lax.fori_loop(
        1, lax.axis_size(axis), lambda source, state: combine(state, take(source)), take(0)
    )


def block_stats(queries, cache_keys, cache_values, visible, score_scale):
    scores = (
        jnp.einsum("bhqd,bhld->bhql", queries, cache_keys, preferred_element_type=jnp.float32)
        * score_scale
    )
    scores = jnp.where(visible, scores, floor_score)
    peak_score = jnp.max(scores, axis=-1)
    weights = jnp.where(visible, jnp.exp(scores - peak_score[..., None]), 0.0)
    weight_total = jnp.sum(weights, axis=-1)
    block_out = jnp.einsum(
        "bhql,bhld->bhqd",
        weights.astype(jnp.bfloat16),
        cache_values,
        preferred_element_type=jnp.float32,
    )
    return (peak_score, weight_total, block_out)


def spread_rows(values_in, selector):
    return jnp.einsum("brq,gr->bgq", values_in, selector, precision=lax.Precision.HIGHEST)


def spread_vectors(values_in, selector):
    return jnp.einsum("brqd,gr->bgqd", values_in, selector, precision=lax.Precision.HIGHEST)


def join_parts(first_part, second_part):
    top_score = jnp.maximum(first_part[0], second_part[0])
    left_factor = jnp.exp(first_part[0] - top_score)
    right_factor = jnp.exp(second_part[0] - top_score)
    joined_total = first_part[1] * left_factor + second_part[1] * right_factor
    joined_out = first_part[2] * left_factor[..., None] + second_part[2] * right_factor[..., None]
    return (top_score, joined_total, joined_out)


def per_device(
    hidden,
    norm_gain,
    q_weight,
    kv_weight,
    out_weight,
    head_kind,
    ret_keys,
    ret_values,
    stream_keys,
    stream_values,
    cache_len,
    sink_len,
    window_len,
):
    requests, drafts, local_width = hidden.shape
    kv_heads = head_kind.shape[0]
    head_dim = ret_keys.shape[3]
    retrieval = ret_keys.shape[1]
    running = stream_keys.shape[1]
    head_count = q_weight.shape[1] // head_dim
    group_size = head_count // kv_heads
    query_rows = drafts * group_size
    devices = lax.axis_size("seq")
    position = lax.axis_index("seq")
    tokens = requests * drafts
    hidden32 = hidden.astype(jnp.float32)
    squares = lax.psum(jnp.sum(hidden32 * hidden32, axis=-1), "seq")
    inverse = lax.rsqrt(squares / (local_width * devices) + epsilon)
    normed = (hidden32 * inverse[..., None] * norm_gain.astype(jnp.float32)).astype(jnp.bfloat16)
    flat_rows = normed.reshape(tokens, local_width)
    part_query = jnp.dot(flat_rows, q_weight, preferred_element_type=jnp.float32)
    part_fresh = jnp.dot(flat_rows, kv_weight, preferred_element_type=jnp.float32)
    whole_query, whole_fresh = lax.psum((part_query, part_fresh), "seq")
    queries = whole_query.astype(jnp.bfloat16)
    new_entries = whole_fresh.astype(jnp.bfloat16)
    grouped = (
        queries.reshape(requests, drafts, kv_heads, group_size, head_dim)
        .transpose(0, 2, 1, 3, 4)
        .reshape(requests, kv_heads, query_rows, head_dim)
    )
    fresh_split = new_entries.reshape(requests, drafts, 2, kv_heads, head_dim)
    new_keys = fresh_split[:, :, 0].transpose(0, 2, 1, 3)
    new_values = fresh_split[:, :, 1].transpose(0, 2, 1, 3)
    kind_flag = head_kind == 1
    rank_ret = jnp.cumsum(head_kind) - 1
    rank_str = jnp.cumsum(1 - head_kind) - 1
    select_ret = (
        kind_flag[:, None] & (rank_ret[:, None] == jnp.arange(retrieval)[None, :])
    ).astype(jnp.float32)
    select_str = (
        jnp.logical_not(kind_flag)[:, None] & (rank_str[:, None] == jnp.arange(running)[None, :])
    ).astype(jnp.float32)
    ret_queries = jnp.einsum(
        "bgqd,gr->brqd",
        grouped,
        select_ret.astype(jnp.bfloat16),
        preferred_element_type=jnp.float32,
    ).astype(jnp.bfloat16)
    str_queries = jnp.einsum(
        "bgqd,gr->brqd",
        grouped,
        select_str.astype(jnp.bfloat16),
        preferred_element_type=jnp.float32,
    ).astype(jnp.bfloat16)
    score_scale = head_dim ** (-0.5)
    cache_block = ret_keys.shape[2]
    cache_pos = position * cache_block + jnp.arange(cache_block)
    ret_visible = (cache_pos[None, :] < cache_len[:, None])[:, None, None, :]
    slot_block = stream_keys.shape[2]
    slot_pos = (position * slot_block + jnp.arange(slot_block))[None, :]
    sink_part = slot_pos < sink_len[:, None]
    recent_part = (slot_pos >= SINK_CAP) & (slot_pos < SINK_CAP + window_len[:, None])
    str_visible = (sink_part | recent_part)[:, None, None, :]
    ret_peak, ret_total, ret_out = block_stats(
        ret_queries, ret_keys, ret_values, ret_visible, score_scale
    )
    str_peak, str_total, str_out = block_stats(
        str_queries, stream_keys, stream_values, str_visible, score_scale
    )
    peak_all = spread_rows(ret_peak, select_ret) + spread_rows(str_peak, select_str)
    total_all = spread_rows(ret_total, select_ret) + spread_rows(str_total, select_str)
    out_all = spread_vectors(ret_out, select_ret) + spread_vectors(str_out, select_str)
    token_of_row = jnp.arange(query_rows) // group_size
    new_visible = jnp.arange(drafts)[None, :] <= token_of_row[:, None]
    new_peak, new_total, new_out = block_stats(
        grouped, new_keys, new_values, new_visible, score_scale
    )
    own_width = out_weight.shape[0]
    cache_peak, cache_total, cache_out = joined((peak_all, total_all, out_all), "seq", join_parts)
    top_score = jnp.maximum(cache_peak, new_peak)
    cache_factor = jnp.exp(cache_peak - top_score)
    new_factor = jnp.exp(new_peak - top_score)
    denominator = cache_total * cache_factor + new_total * new_factor
    attended = (
        cache_out * cache_factor[..., None] + new_out * new_factor[..., None]
    ) / denominator[..., None]
    attention = (
        attended.reshape(requests, kv_heads, drafts, group_size, head_dim)
        .transpose(0, 2, 1, 3, 4)
        .reshape(tokens, head_count * head_dim)
        .astype(jnp.bfloat16)
    )
    own_attention = lax.dynamic_slice_in_dim(attention, position * own_width, own_width, 1)
    own_output = lax.psum_scatter(
        lax.dot_general(
            out_weight, own_attention, (((0,), (1,)), ((), ())), preferred_element_type=jnp.float32
        ),
        "seq",
        scatter_dimension=0,
        tiled=True,
    )
    layer_output = own_output.T.reshape(requests, drafts, local_width).astype(jnp.bfloat16)
    return (layer_output, new_entries.reshape(requests, drafts, 2 * kv_heads * head_dim))


def solution(mesh):
    in_specs = (
        P("groups", None, "seq"),
        P("seq"),
        P("seq", None),
        P("seq", None),
        P("seq", None),
        P(),
        P("groups", None, "seq", None),
        P("groups", None, "seq", None),
        P("groups", None, "seq", None),
        P("groups", None, "seq", None),
        P("groups"),
        P("groups"),
        P("groups"),
    )
    out_specs = (P("groups", None, "seq"), P("groups", None, None))
    return jax.shard_map(
        per_device, mesh=mesh, in_specs=in_specs, out_specs=out_specs, check_vma=False
    )
```

profile of v0, /device:TPU:0, one launch (start us, length us, event | category | flops | bytes accessed | tf_op | source)
XLA Modules:
  0.0 258.6 jit_solution(16587945270876655756)
XLA Ops:
  11.2 34.9 %psum.21 = f32[2,4]{1,0:T(2,128)S(1)} all-reduce(f32[2,4]{1,0:T(2,128)S(1)} %fusion.37), channel_id=1, replica_groups=mesh['groups'=2,'seq'=16] {'seq'}, use_global_device_ids=true, to_apply=%region_2.0 | all-reduce | flops 8 | bytes 64 | tf_op jit(solution)/shard_map/psum | solution.py:86
  48.0 4.6 %fusion.73 = f32[8,8192]{1,0:T(8,128)S(1)} fusion(bf16[8,512]{1,0:T(8,128)(2,1)S(1)} %reshape.194, bf16[512,8192]{1,0:T(8,128)(2,1)} %param.17), kind=kOutput, calls=%fused_computation.113 | convolution fusion | flops 67108864 | bytes 8658944 | tf_op jit(solution)/shard_map/dot_general | solution.py:90
  52.6 60.7 %all-reduce.2 = (bf16[8,8192]{1,0:T(8,128)(2,1)S(1)}, bf16[8,2048]{1,0:T(8,128)(2,1)S(1)}) all-reduce(f32[8,8192]{1,0:T(8,128)S(1)} %fusion.73, f32[8,2048]{1,0:T(8,128)S(1)} %fusion.74), channel_id=1, replica_groups=mesh['groups'=2,'seq'=16] {'seq'}, use_global_device_ids=true, to_apply=%region_3.0 | all-reduce | flops 81920 | bytes 491520 | tf_op jit(solution)/shard_map/psum | solution.py:92
  113.7 3.9 %fusion.70 = (f32[2,4,32]{2,1,0:T(4,128)S(1)}, f32[2,4,32,2048]{3,2,1,0:T(8,128)S(1)}) fusion(bf16[2,4,2048,128]{3,2,1,0:T(8,128)(2,1)} %param.21, bf16[2,4,32,128]{3,1,2,0:T(4,128)(2,1)S(1)} %fusion.12, pred[2,2048]{1,0:T(4,128)(4,1)S(1)} %broadcast_compare_fusion), kind=kOutput, calls=%fused_computation.110 | convolution fusion | flops 135790336 | bytes 6362112 | tf_op jit(solution)/shard_map/bhqd,bhld->bhql/dot_general | solution.py:26
  121.5 2.1 fusion.5
  124.0 17.6 %all-gather.1 = f32[32,8,32]{2,1,0:T(8,128)S(1)} all-gather(f32[2,8,32]{2,1,0:T(8,128)S(1)} %fusion.15), channel_id=3, replica_groups=mesh['groups'=2,'seq'=16] {'seq'}, dimensions={0}, use_global_device_ids=true | all-gather | bytes 34816 | tf_op jit(solution)/shard_map/all_gather | solution.py:14
  142.0 20.1 %all-gather = f32[32,8,32]{2,1,0:T(8,128)S(1)} all-gather(f32[2,8,32]{2,1,0:T(8,128)S(1)} %fusion.16), channel_id=2, replica_groups=mesh['groups'=2,'seq'=16] {'seq'}, dimensions={0}, use_global_device_ids=true | all-gather | bytes 34816 | tf_op jit(solution)/shard_map/all_gather | solution.py:14
  162.4 7.8 %all-gather.5.cloned.1.call-done = f32[32,8,32,128]{3,2,1,0:T(8,128)} async-done(((f32[2,8,32,128]{3,2,1,0:T(8,128)}), f32[32,8,32,128]{3,2,1,0:T(8,128)}) %all-gather.5.cloned.1.call-update) | async-done | bytes 4194320 | tf_op jit(solution)/shard_map/all_gather | solution.py:14
  171.2 18.9 %while.19 = (s32[]{:T(128)}, f32[2,8,32]{2,1,0:T(8,128)S(1)}, f32[2,8,32]{2,1,0:T(8,128)S(1)}, f32[2,8,32,128]{3,2,1,0:T(8,128)S(1)}, f32[16,2,8,32]{3,2,1,0:T(8...) while((s32[]{:T(128)}, f32[2,8,32]{2,1,0:T(8,128)S(1)}, ...), condition=%wide.region_10.11_spmd, body=%wide.region_9.10_spmd.sunk | while | flops 199685 | bytes 807055 | solution.py:19
  171.2 1.2 fusion.93
  172.5 1.2 fusion.93
  173.7 1.2 fusion.93
  175.0 1.2 fusion.93
  176.3 1.2 fusion.93
  177.5 1.2 fusion.93
  178.8 1.2 fusion.93
  180.1 1.2 fusion.93
  181.3 1.2 fusion.93
  182.6 1.2 fusion.93
  186.4 1.2 fusion.93
  187.6 1.2 fusion.93
  188.9 1.2 fusion.93
  190.6 5.3 %convolution_bitcast_fusion = f32[8192,8]{0,1:T(8,128)} fusion(bf16[512,8192]{1,0:T(8,128)(2,1)} %param.19, bf16[8,8192]{1,0:T(8,128)(2,1)S(1)} %convert_element_type.88, s32[]{:T(128)S(6)} %select_n.59), kind=kOutput, calls=%fused_computation.8 | convolution fusion | flops 67108864 | bytes 8658948 | tf_op jit(solution)/shard_map/dot_general | solution.py:164
  196.6 53.8 %reduce-scatter.2.cloned.1.call-done = f32[512,8]{0,1:T(8,128)} async-done(((f32[8192,8]{0,1:T(8,128)}), f32[512,8]{0,1:T(8,128)}) %reduce-scatter.2.cloned.1.call-update) | async-done | bytes 16400 | tf_op jit(solution)/shard_map/reduce_scatter | solution.py:163
  (85 shorter events, 17.1 us)
Async XLA Ops:
  7.2 40.4 %copy-start = (bf16[512,2048]{1,0:T(8,128)(2,1)S(1)}, bf16[512,2048]{1,0:T(8,128)(2,1)}, u32[]{:S(2)}) copy-start(bf16[512,2048]{1,0:T(8,128)(2,1)} %param.18) | copy-start | bytes 6291460
  7.2 163.0 %all-gather.5.cloned.1.call-start = ((), (), s32[]{:S(2)}) async-start(), calls=%async_computation.2 | async-start | bytes 4456448 | tf_op jit(solution)/shard_map/all_gather | solution.py:14
  48.0 65.7 %copy-start.5 = (s32[2]{0:T(128)S(1)}, s32[2]{0:T(128)}, u32[]{:S(2)}) copy-start(s32[2]{0:T(128)} %param.25) | copy-start | bytes 28
  113.7 4.0 %copy-start.2 = (bf16[2,4,2048,128]{3,2,1,0:T(8,128)(2,1)S(1)}, bf16[2,4,2048,128]{3,2,1,0:T(8,128)(2,1)}, u32[]{:S(2)}) copy-start(bf16[2,4,2048,128]{3,2,1,0:T(8,128)(2,1)} %param.22) | copy-start | bytes 12582916
  117.7 1.3 copy-start.1
  117.7 1.7 copy-start.6
  117.7 1.8 copy-start.4
  117.7 2.1 copy-start.3
  121.2 129.2 %reduce-scatter.2.cloned.1.call-start = ((), (), s32[]{:S(2)}) async-start(), calls=%async_computation.1 | async-start | bytes 278528 | tf_op jit(solution)/shard_map/reduce_scatter | solution.py:163
Sparse Core Ops, SparseCore 0:
  121.3 48.8 all-gather.4
  196.0 54.3 reduce-scatter.1
where the time goes:
time: 260 us; the launch traced here: 259 us
  blocking collectives  133 us (51%)
  waiting for transfers between devices  61.7 us (24%)
  other arithmetic  27.2 us (10%)
  matrix products  18 us (7%)
  between operations  14.3 us (6%)
  local copies, waits for them, and re-layouts  3.58 us (1%)
    psum x1, blocking collectives, per_device(): whole_query, whole_fresh = lax.psum((part_query, part_fresh), 'seq')  60.7 us
    reduce_scatter x1, waiting for transfers between devices, per_device(): lax.psum_scatter(lax.dot_general(out_weight, own_attention, (((0,), (1,))...  53.8 us
    all_gather x2, blocking collectives, joined(): gathered = jax.tree.map(lambda a: lax.all_gather(a, axis), part)  37.7 us
    psum x1, blocking collectives, per_device(): squares = lax.psum(jnp.sum(hidden32 * hidden32, axis=-1), 'seq')  34.9 us
    add x15, other arithmetic, join_parts(): first_part[2] * left_factor[..., None]  18.2 us
    all_gather x1, waiting for transfers between devices, joined(): gathered = jax.tree.map(lambda a: lax.all_gather(a, axis), part)  7.8 us
    dot_general x1, matrix products, per_device(): lax.dot_general(out_weight, own_attention, (((0,), (1,)), ((), ())), pref...  5.28 us
  transfers between devices with their start and end apart: 2, of which 2 were waited for; matrix products, arithmetic and copies ran while one was open for 2% of the time, Pallas kernels for 0%

commit v1 on v0

--- a/solution.py
+++ b/solution.py
@@ -10,15 +10,21 @@
 floor_score = -1e30
 
 
-def joined(part, axis, combine):
-    gathered = jax.tree.map(lambda a: lax.all_gather(a, axis), part)
-
-    def take(source):
-        return jax.tree.map(lambda a: lax.dynamic_index_in_dim(a, source, 0, False), gathered)
-
-    return lax.fori_loop(
-        1, lax.axis_size(axis), lambda source, state: combine(state, take(source)), take(0)
-    )
+def exchanged(parts):
+    return lax.all_to_all(parts, "seq", 0, 0, tiled=True)
+
+
+def summed_over_devices(value):
+    devices = lax.axis_size("seq")
+    step = 1
+    while step < devices:
+        value = value + lax.ppermute(value, "seq", [(i, i ^ step) for i in range(devices)])
+        step *= 2
+    return value
+
+
+def column_blocks(rows, blocks):
+    return rows.reshape(rows.shape[0], blocks, -1).transpose(1, 0, 2)
 
 
 def block_stats(queries, cache_keys, cache_values, visible, score_scale):
@@ -45,15 +51,6 @@
 
 def spread_vectors(values_in, selector):
     return jnp.einsum("brqd,gr->bgqd", values_in, selector, precision=lax.Precision.HIGHEST)
-
-
-def join_parts(first_part, second_part):
-    top_score = jnp.maximum(first_part[0], second_part[0])
-    left_factor = jnp.exp(first_part[0] - top_score)
-    right_factor = jnp.exp(second_part[0] - top_score)
-    joined_total = first_part[1] * left_factor + second_part[1] * right_factor
-    joined_out = first_part[2] * left_factor[..., None] + second_part[2] * right_factor[..., None]
-    return (top_score, joined_total, joined_out)
 
 
 def per_device(
@@ -83,15 +80,24 @@
     position = lax.axis_index("seq")
     tokens = requests * drafts
     hidden32 = hidden.astype(jnp.float32)
-    squares = lax.psum(jnp.sum(hidden32 * hidden32, axis=-1), "seq")
+    squares = summed_over_devices(jnp.sum(hidden32 * hidden32, axis=-1))
     inverse = lax.rsqrt(squares / (local_width * devices) + epsilon)
     normed = (hidden32 * inverse[..., None] * norm_gain.astype(jnp.float32)).astype(jnp.bfloat16)
     flat_rows = normed.reshape(tokens, local_width)
     part_query = jnp.dot(flat_rows, q_weight, preferred_element_type=jnp.float32)
     part_fresh = jnp.dot(flat_rows, kv_weight, preferred_element_type=jnp.float32)
-    whole_query, whole_fresh = lax.psum((part_query, part_fresh), "seq")
-    queries = whole_query.astype(jnp.bfloat16)
-    new_entries = whole_fresh.astype(jnp.bfloat16)
+    sums = jnp.sum(
+        exchanged(
+            jnp.concatenate(
+                [column_blocks(part_query, devices), column_blocks(part_fresh, devices)], axis=-1
+            )
+        ),
+        axis=0,
+    ).astype(jnp.bfloat16)
+    gathered = exchanged(jnp.broadcast_to(sums[None], (devices, *sums.shape)))
+    query_width = q_weight.shape[1] // devices
+    queries = gathered[..., :query_width].transpose(1, 0, 2).reshape(tokens, -1)
+    new_entries = gathered[..., query_width:].transpose(1, 0, 2).reshape(tokens, -1)
     grouped = (
         queries.reshape(requests, drafts, kv_heads, group_size, head_dim)
         .transpose(0, 2, 1, 3, 4)
@@ -145,30 +151,51 @@
         grouped, new_keys, new_values, new_visible, score_scale
     )
     own_width = out_weight.shape[0]
-    cache_peak, cache_total, cache_out = joined((peak_all, total_all, out_all), "seq", join_parts)
-    top_score = jnp.maximum(cache_peak, new_peak)
-    cache_factor = jnp.exp(cache_peak - top_score)
-    new_factor = jnp.exp(new_peak - top_score)
-    denominator = cache_total * cache_factor + new_total * new_factor
+    block_heads = max(1, own_width // head_dim)
+
+    def by_token(value):
+        split = value.reshape(requests, kv_heads, drafts, group_size, -1)
+        return split.transpose(0, 2, 1, 3, 4).reshape(tokens, head_count, -1)
+
+    first_head = (jnp.arange(devices) * own_width) // head_dim
+    block_head = first_head[:, None] + jnp.arange(block_heads)[None, :]
+
+    def head_blocks(value):
+        rows = by_token(value).reshape(tokens, head_count)
+        return jnp.take(rows, block_head.reshape(-1), axis=1).reshape(tokens, devices, -1).transpose(1, 0, 2)
+
+    received = exchanged(
+        jnp.concatenate(
+            [
+                column_blocks(by_token(out_all).reshape(tokens, -1), devices),
+                head_blocks(peak_all),
+                head_blocks(total_all),
+            ],
+            axis=-1,
+        )
+    )
+    got_out = received[..., :own_width].reshape(devices, tokens, block_heads, -1)
+    got_peak = received[..., own_width : own_width + block_heads]
+    got_total = received[..., own_width + block_heads :]
+
+    def own_heads(value):
+        blocks = column_blocks(by_token(value).reshape(tokens, -1), devices)
+        return lax.dynamic_index_in_dim(blocks, position, 0, False).reshape(tokens, block_heads, -1)
+
+    own_new_out = own_heads(new_out)
+    own_new_peak = lax.dynamic_index_in_dim(head_blocks(new_peak), position, 0, False)
+    own_new_total = lax.dynamic_index_in_dim(head_blocks(new_total), position, 0, False)
+    top_score = jnp.maximum(jnp.max(got_peak, axis=0), own_new_peak)
+    cache_factor = jnp.exp(got_peak - top_score[None])
+    new_factor = jnp.exp(own_new_peak - top_score)
+    denominator = jnp.sum(got_total * cache_factor, axis=0) + own_new_total * new_factor
     attended = (
-        cache_out * cache_factor[..., None] + new_out * new_factor[..., None]
+        jnp.sum(got_out * cache_factor[..., None], axis=0) + own_new_out * new_factor[..., None]
     ) / denominator[..., None]
-    attention = (
-        attended.reshape(requests, kv_heads, drafts, group_size, head_dim)
-        .transpose(0, 2, 1, 3, 4)
-        .reshape(tokens, head_count * head_dim)
-        .astype(jnp.bfloat16)
-    )
-    own_attention = lax.dynamic_slice_in_dim(attention, position * own_width, own_width, 1)
-    own_output = lax.psum_scatter(
-        lax.dot_general(
-            out_weight, own_attention, (((0,), (1,)), ((), ())), preferred_element_type=jnp.float32
-        ),
-        "seq",
-        scatter_dimension=0,
-        tiled=True,
-    )
-    layer_output = own_output.T.reshape(requests, drafts, local_width).astype(jnp.bfloat16)
+    own_attention = attended.reshape(tokens, own_width).astype(jnp.bfloat16)
+    part_output = jnp.dot(own_attention, out_weight, preferred_element_type=jnp.float32)
+    own_output = jnp.sum(exchanged(column_blocks(part_output, devices)), axis=0)
+    layer_output = own_output.reshape(requests, drafts, local_width).astype(jnp.bfloat16)
     return (layer_output, new_entries.reshape(requests, drafts, 2 * kv_heads * head_dim))
 
 

time: 260 us -> 124 us (0.48)
  blocking collectives: 133 us -> 0 us
  local copies, waits for them, and re-layouts: 3.58 us -> 34.7 us
  waiting for transfers between devices: 61.7 us -> 33.4 us
  starting transfers between devices: 0.08 us -> 27.4 us
  other arithmetic: 27.2 us -> 5.78 us
  between operations: 14.3 us -> 1.05 us
    psum x2 -> x0, blocking collectives: 95.6 us -> none  [the longest x1 60.7 us: per_device(): whole_query, whole_fresh = lax.psum((part_query, part_fresh), 'seq')]
    reduce_scatter x1 -> x0, waiting for transfers between devices: 53.8 us -> none  [per_device(): lax.psum_scatter(lax.dot_general(out_weight, own_attention, (((0,), (1,))...]
    all_gather x2 -> x0, blocking collectives: 37.7 us -> none  [joined(): gathered = jax.tree.map(lambda a: lax.all_gather(a, axis), part)]
    all_to_all x0 -> x4, waiting for transfers between devices: none -> 28.7 us  [exchanged(): return lax.all_to_all(parts, 'seq', 0, 0, tiled=True)]
    dot_general x0 -> x3, local copies, waits for them, and re-layouts: none -> 26.8 us  [the longest x1 12 us: per_device(): jnp.dot(own_attention, out_weight, preferred_element_type=jnp.float32)]
    all_to_all x0 -> x4, starting transfers between devices: none -> 19.3 us  [exchanged(): return lax.all_to_all(parts, 'seq', 0, 0, tiled=True)]
    add x31 -> x5, other arithmetic: 18.5 us -> 0.09 us  [the longest x1 0.07 us: per_device(): block_head = first_head[:, None] + jnp.arange(block_heads)[None, :]]
    ppermute x0 -> x4, starting transfers between devices: none -> 8.18 us  [summed_over_devices(): lax.ppermute(value, 'seq', [(i, i ^ step) for i in range(devices)])]
  transfers between devices with their start and end apart: 2 -> 8, of which waited for: 2 -> 6; matrix products, arithmetic and copies ran while one was open for 2% -> 25% of each run, Pallas kernels for 0% -> 0%
where the time goes in v1:
time: 124 us; the launch traced here: 123 us
  local copies, waits for them, and re-layouts  34.7 us (28%)
  waiting for transfers between devices  33.4 us (27%)
  starting transfers between devices  27.4 us (22%)
  matrix products  20.2 us (16%)
  other arithmetic  5.78 us (5%)
    all_to_all x4, waiting for transfers between devices, exchanged(): return lax.all_to_all(parts, 'seq', 0, 0, tiled=True)  28.7 us
    all_to_all x4, starting transfers between devices, exchanged(): return lax.all_to_all(parts, 'seq', 0, 0, tiled=True)  19.3 us
    dot_general x1, local copies, waits for them, and re-layouts, per_device(): jnp.dot(own_attention, out_weight, preferred_element_type=jnp.float32)  12 us
    dot_general x1, local copies, waits for them, and re-layouts, per_device(): jnp.dot(flat_rows, q_weight, preferred_element_type=jnp.float32)  11.9 us
    ppermute x4, starting transfers between devices, summed_over_devices(): lax.ppermute(value, 'seq', [(i, i ^ step) for i in range(devices)])  8.18 us
    dot_general x1, matrix products, per_device(): jnp.dot(own_attention, out_weight, preferred_element_type=jnp.float32)  6.37 us
    dot_general x1, matrix products, per_device(): jnp.dot(flat_rows, q_weight, preferred_element_type=jnp.float32)  5.64 us
    ppermute x4, waiting for transfers between devices, summed_over_devices(): lax.ppermute(value, 'seq', [(i, i ^ step) for i in range(devices)])  4.66 us
  transfers between devices with their start and end apart: 8, of which 6 were waited for; matrix products, arithmetic and copies ran while one was open for 25% of the time, Pallas kernels for 0%

profile of v1, /device:TPU:0, one launch (start us, length us, event | category | flops | bytes accessed | tf_op | source)
XLA Modules:
  0.0 122.5 jit_solution(16375369530517597932)
XLA Ops:
  0.6 0.8 fusion.30
  3.5 0.7 convert_element_type.70
  4.2 11.9 %copy.145 = bf16[8192,512]{1,0:T(8,128)(2,1)} copy(bf16[8192,512]{0,1:T(8,128)(2,1)} %bitcast.176) | data formatting | bytes 16777216 | tf_op jit(solution)/shard_map/dot_general | solution.py:87
  16.2 2.9 %copy.146 = bf16[2048,512]{1,0:T(8,128)(2,1)S(1)} copy(bf16[2048,512]{0,1:T(8,128)(2,1)} %bitcast.179) | data formatting | bytes 4194304 | tf_op jit(solution)/shard_map/dot_general | solution.py:88
  19.6 2.5 %collective-permute-start.1 = (f32[2,4]{1,0:T(2,128)S(1)}, f32[2,4]{1,0:T(2,128)S(1)}, u32[]{:S(2)}, u32[]{:S(2)}) collective-permute-start(f32[2,4]{1,0:T(2,128)S(1)} %add.156), channel_id=1, source_target_pairs={{0,2},{1,3},{2,0},{3,1},{4,6},{5,7},{6,4},{7,5},{8,10},{9,11},{10,... | collective-permute-start | bytes 104 | tf_op jit(solution)/shard_map/ppermute | solution.py:21
  22.1 1.6 %collective-permute-done.1 = f32[2,4]{1,0:T(2,128)S(1)} collective-permute-done((f32[2,4]{1,0:T(2,128)S(1)}, f32[2,4]{1,0:T(2,128)S(1)}, u32[]{:S(2)}, u32[]{:S(2)}) %collective-permute-start.1) | collective-permute-done | bytes 64 | tf_op jit(solution)/shard_map/ppermute | solution.py:21
  23.7 2.1 %collective-permute-start.2 = (f32[2,4]{1,0:T(2,128)S(1)}, f32[2,4]{1,0:T(2,128)S(1)}, u32[]{:S(2)}, u32[]{:S(2)}) collective-permute-start(f32[2,4]{1,0:T(2,128)S(1)} %add.157), channel_id=1, source_target_pairs={{0,4},{1,5},{2,6},{3,7},{4,0},{5,1},{6,2},{7,3},{8,12},{9,13},{10,... | collective-permute-start | bytes 104 | tf_op jit(solution)/shard_map/ppermute | solution.py:21
  25.8 1.6 %collective-permute-done.2 = f32[2,4]{1,0:T(2,128)S(1)} collective-permute-done((f32[2,4]{1,0:T(2,128)S(1)}, f32[2,4]{1,0:T(2,128)S(1)}, u32[]{:S(2)}, u32[]{:S(2)}) %collective-permute-start.2) | collective-permute-done | bytes 64 | tf_op jit(solution)/shard_map/ppermute | solution.py:21
  27.3 3.0 %collective-permute-start.3 = (f32[2,4]{1,0:T(2,128)S(1)}, f32[2,4]{1,0:T(2,128)S(1)}, u32[]{:S(2)}, u32[]{:S(2)}) collective-permute-start(f32[2,4]{1,0:T(2,128)S(1)} %add.158), channel_id=1, source_target_pairs={{0,8},{1,9},{2,10},{3,11},{4,12},{5,13},{6,14},{7,15},{8,0},{9,1},... | collective-permute-start | bytes 104 | tf_op jit(solution)/shard_map/ppermute | solution.py:21
  30.4 1.6 %collective-permute-done.3 = f32[2,4]{1,0:T(2,128)S(1)} collective-permute-done((f32[2,4]{1,0:T(2,128)S(1)}, f32[2,4]{1,0:T(2,128)S(1)}, u32[]{:S(2)}, u32[]{:S(2)}) %collective-permute-start.3) | collective-permute-done | bytes 64 | tf_op jit(solution)/shard_map/ppermute | solution.py:21
  32.0 5.6 %convolution_bitcast_fusion.1 = f32[16,8,512]{2,1,0:T(8,128)S(1)} fusion(bf16[8,512,1]{1,0,2:T(8,128)(2,1)S(1)} %reshape.377, bf16[16,512,512]{2,1,0:T(8,128)(2,1)} %bitcast.175), kind=kOutput, calls=%fused_computation.10 | convolution fusion | flops 67108864 | bytes 8658944 | tf_op jit(solution)/shard_map/dot_general | solution.py:87
  38.3 0.8 pad_maximum_fusion
  39.1 6.2 %all-to-all-start = ((f32[16,8,640]{2,1,0:T(8,128)}), f32[16,8,640]{2,1,0:T(8,128)S(1)}, u32[]{:S(2)}, u32[]{:S(2)}) async-start(f32[16,8,640]{2,1,0:T(8,128)} %pad_maximum_fusion), calls=%async_computation | async-start | bytes 655360 | tf_op jit(solution)/shard_map/all_to_all | solution.py:14
  45.4 10.9 %all-to-all-done = f32[16,8,640]{2,1,0:T(8,128)S(1)} async-done(((f32[16,8,640]{2,1,0:T(8,128)}), f32[16,8,640]{2,1,0:T(8,128)S(1)}, u32[]{:S(2)}, u32[]{:S(2)}) %all-to-all-start) | async-done | bytes 327712 | tf_op jit(solution)/shard_map/all_to_all | solution.py:14
  57.1 3.5 %all-to-all-start.1 = ((bf16[16,8,640]{2,1,0:T(8,128)(2,1)}), bf16[16,8,640]{2,1,0:T(8,128)(2,1)S(1)}, u32[]{:S(2)}, u32[]{:S(2)}) async-start(bf16[16,8,640]{2,1,0:T(8,128)(2,1)} %broadcast_in_dim.92), calls=%async_computation.1 | async-start | bytes 327680 | tf_op jit(solution)/shard_map/all_to_all | solution.py:14
  60.6 8.4 %all-to-all-done.1 = bf16[16,8,640]{2,1,0:T(8,128)(2,1)S(1)} async-done(((bf16[16,8,640]{2,1,0:T(8,128)(2,1)}), bf16[16,8,640]{2,1,0:T(8,128)(2,1)S(1)}, u32[]{:S(2)}, u32[]{:S(2)}) %all-to-all-start.1) | async-done | bytes 163872 | tf_op jit(solution)/shard_map/all_to_all | solution.py:14
  70.3 3.9 %fusion.63 = (f32[2,4,32]{2,1,0:T(4,128)S(1)}, f32[2,4,32,2048]{3,2,1,0:T(8,128)S(1)}) fusion(bf16[2,4,2048,128]{3,2,1,0:T(8,128)(2,1)} %param.21, bf16[2,4,32,128]{3,1,2,0:T(4,128)(2,1)S(1)} %fusion.4, pred[2,2048]{1,0:T(4,128)(4,1)S(1)} %broadcast_compare_fusion), kind=kOutput, calls=%fused_computation.130 | convolution fusion | flops 135790336 | bytes 6362112 | tf_op jit(solution)/shard_map/bhqd,bhld->bhql/dot_general | solution.py:32
  75.0 0.9 fusion.9
  81.5 0.9 copy.118
  82.4 3.5 %all-to-all-start.2 = ((f32[16,8,520]{2,1,0:T(8,128)}), f32[16,8,520]{2,1,0:T(8,128)S(1)}, u32[]{:S(2)}, u32[]{:S(2)}) async-start(f32[16,8,520]{2,1,0:T(8,128)} %copy.118), calls=%async_computation.2 | async-start | bytes 655360 | tf_op jit(solution)/shard_map/all_to_all | solution.py:14
  85.9 12.0 %copy.147 = bf16[8192,512]{1,0:T(8,128)(2,1)} copy(bf16[8192,512]{0,1:T(8,128)(2,1)} %bitcast.177) | data formatting | bytes 16777216 | tf_op jit(solution)/shard_map/dot_general | solution.py:196
  99.5 6.4 %convolution_bitcast_fusion = f32[16,8,512]{2,1,0:T(8,128)} fusion(bf16[16,512,512]{2,1,0:T(8,128)(2,1)} %bitcast.174, f32[8,512]{1,0:T(8,128)S(1)} %fusion.14, f32[8,1,512]{2,1,0:T(1,128)S(1)} %constant_dynamic-slice_fusion, f32[8,4]{0,1:T(4,128)S(1)} %copy.139, f32[8,4]{0,1:T(4,128)S(1)} %copy.133), kind=kOutput, calls=%fused_computation.9 | convolution fusion | flops 67125248 | bytes 8683776 | tf_op jit(solution)/shard_map/dot_general | solution.py:196
  105.9 6.0 %all-to-all-start.3 = ((f32[16,8,512]{2,1,0:T(8,128)}), f32[16,8,512]{2,1,0:T(8,128)S(1)}, u32[]{:S(2)}, u32[]{:S(2)}) async-start(f32[16,8,512]{2,1,0:T(8,128)} %convolution_bitcast_fusion), calls=%async_computation.3 | async-start | bytes 524288 | tf_op jit(solution)/shard_map/all_to_all | solution.py:14
  112.5 9.4 %all-to-all-done.3 = f32[16,8,512]{2,1,0:T(8,128)S(1)} async-done(((f32[16,8,512]{2,1,0:T(8,128)}), f32[16,8,512]{2,1,0:T(8,128)S(1)}, u32[]{:S(2)}, u32[]{:S(2)}) %all-to-all-start.3) | async-done | bytes 262176 | tf_op jit(solution)/shard_map/all_to_all | solution.py:14
  (119 shorter events, 14.4 us)
Async XLA Ops:
  0.6 68.7 %copy-start = (bf16[2,4,128,128]{3,2,1,0:T(8,128)(2,1)S(1)}, bf16[2,4,128,128]{3,2,1,0:T(8,128)(2,1)}, u32[]{:S(2)}) copy-start(bf16[2,4,128,128]{3,2,1,0:T(8,128)(2,1)} %param.23) | copy-start | bytes 786436
  1.5 18.1 %collective-permute-start = (f32[2,4]{1,0:T(2,128)S(1)}, f32[2,4]{1,0:T(2,128)S(1)}, u32[]{:S(2)}, u32[]{:S(2)}) collective-permute-start(f32[2,4]{1,0:T(2,128)S(1)} %fusion.30), channel_id=1, source_target_pairs={{0,1},{1,0},{2,3},{3,2},{4,5},{5,4},{6,7},{7,6},{8,9},{9,8},{10,11... | collective-permute-start | bytes 104 | tf_op jit(solution)/shard_map/ppermute | solution.py:21
  16.1 3.1 %copy-start.6 = (s32[8]{0:T(128)S(1)}, s32[8]{0:T(128)}, u32[]{:S(2)}) copy-start(s32[8]{0:T(128)} %param.20) | copy-start | bytes 100
  16.1 3.3 %copy-start.7 = (s32[2]{0:T(128)S(1)}, s32[2]{0:T(128)}, u32[]{:S(2)}) copy-start(s32[2]{0:T(128)} %param.27) | copy-start | bytes 28
  16.2 3.3 %copy-start.4 = (s32[2]{0:T(128)S(1)}, s32[2]{0:T(128)}, u32[]{:S(2)}) copy-start(s32[2]{0:T(128)} %param.26) | copy-start | bytes 28
  16.2 15.8 %copy-start.3 = (bf16[2,4,512]{2,1,0:T(4,128)(2,1)S(1)}, bf16[2,4,512]{2,1,0:T(4,128)(2,1)}, u32[]{:S(2)}) copy-start(bf16[2,4,512]{2,1,0:T(4,128)(2,1)} %param.15) | copy-start | bytes 24580
  19.6 4.1 %collective-permute-start.1 = (f32[2,4]{1,0:T(2,128)S(1)}, f32[2,4]{1,0:T(2,128)S(1)}, u32[]{:S(2)}, u32[]{:S(2)}) collective-permute-start(f32[2,4]{1,0:T(2,128)S(1)} %add.156), channel_id=1, source_target_pairs={{0,2},{1,3},{2,0},{3,1},{4,6},{5,7},{6,4},{7,5},{8,10},{9,11},{10,... | collective-permute-start | bytes 104 | tf_op jit(solution)/shard_map/ppermute | solution.py:21
  23.7 3.7 %collective-permute-start.2 = (f32[2,4]{1,0:T(2,128)S(1)}, f32[2,4]{1,0:T(2,128)S(1)}, u32[]{:S(2)}, u32[]{:S(2)}) collective-permute-start(f32[2,4]{1,0:T(2,128)S(1)} %add.157), channel_id=1, source_target_pairs={{0,4},{1,5},{2,6},{3,7},{4,0},{5,1},{6,2},{7,3},{8,12},{9,13},{10,... | collective-permute-start | bytes 104 | tf_op jit(solution)/shard_map/ppermute | solution.py:21
  27.3 4.6 %collective-permute-start.3 = (f32[2,4]{1,0:T(2,128)S(1)}, f32[2,4]{1,0:T(2,128)S(1)}, u32[]{:S(2)}, u32[]{:S(2)}) collective-permute-start(f32[2,4]{1,0:T(2,128)S(1)} %add.158), channel_id=1, source_target_pairs={{0,8},{1,9},{2,10},{3,11},{4,12},{5,13},{6,14},{7,15},{8,0},{9,1},... | collective-permute-start | bytes 104 | tf_op jit(solution)/shard_map/ppermute | solution.py:21
  37.6 7.7 %copy-start.5 = (s32[2]{0:T(128)S(1)}, s32[2]{0:T(128)}, u32[]{:S(2)}) copy-start(s32[2]{0:T(128)} %param.25) | copy-start | bytes 28
  38.3 31.6 %copy-start.2 = (bf16[2,4,128,128]{3,2,1,0:T(8,128)(2,1)S(1)}, bf16[2,4,128,128]{3,2,1,0:T(8,128)(2,1)}, u32[]{:S(2)}) copy-start(bf16[2,4,128,128]{3,2,1,0:T(8,128)(2,1)} %param.24) | copy-start | bytes 786436
  39.1 17.3 %all-to-all-start = ((f32[16,8,640]{2,1,0:T(8,128)}), f32[16,8,640]{2,1,0:T(8,128)S(1)}, u32[]{:S(2)}, u32[]{:S(2)}) async-start(f32[16,8,640]{2,1,0:T(8,128)} %pad_maximum_fusion), calls=%async_computation | async-start | bytes 655360 | tf_op jit(solution)/shard_map/all_to_all | solution.py:14
  57.1 11.9 %all-to-all-start.1 = ((bf16[16,8,640]{2,1,0:T(8,128)(2,1)}), bf16[16,8,640]{2,1,0:T(8,128)(2,1)S(1)}, u32[]{:S(2)}, u32[]{:S(2)}) async-start(bf16[16,8,640]{2,1,0:T(8,128)(2,1)} %broadcast_in_dim.92), calls=%async_computation.1 | async-start | bytes 327680 | tf_op jit(solution)/shard_map/all_to_all | solution.py:14
  70.3 4.7 %copy-start.1 = (bf16[2,4,2048,128]{3,2,1,0:T(8,128)(2,1)S(1)}, bf16[2,4,2048,128]{3,2,1,0:T(8,128)(2,1)}, u32[]{:S(2)}) copy-start(bf16[2,4,2048,128]{3,2,1,0:T(8,128)(2,1)} %param.22) | copy-start | bytes 12582916
  82.4 16.0 %all-to-all-start.2 = ((f32[16,8,520]{2,1,0:T(8,128)}), f32[16,8,520]{2,1,0:T(8,128)S(1)}, u32[]{:S(2)}, u32[]{:S(2)}) async-start(f32[16,8,520]{2,1,0:T(8,128)} %copy.118), calls=%async_computation.2 | async-start | bytes 655360 | tf_op jit(solution)/shard_map/all_to_all | solution.py:14
  105.9 16.0 %all-to-all-start.3 = ((f32[16,8,512]{2,1,0:T(8,128)}), f32[16,8,512]{2,1,0:T(8,128)S(1)}, u32[]{:S(2)}, u32[]{:S(2)}) async-start(f32[16,8,512]{2,1,0:T(8,128)} %convolution_bitcast_fusion), calls=%async_computation.3 | async-start | bytes 524288 | tf_op jit(solution)/shard_map/all_to_all | solution.py:14
